TPU v7x, 32 devices: a whole 2x2x4 slice. The times are simulated.
32 devices in a mesh: scan: 2 (over x), seq: 16 (over z, y, core).
Axes of the slice: x: 2, y: 2, z: 4, core: 2. Of those that a mesh axis runs over, the one named last changes fastest.
Arguments:
- tokens: bfloat16 [8192, 1024], P(('scan', 'seq')), parts along dimension 0, may hold values from -12 to 12
- ln_gain: float32 [1024], replicated, may hold values from 0.1 to 1.9
- w_query: bfloat16 [1024, 1024], P('seq'), may hold values from -2 to 2
- w_key: bfloat16 [1024, 1024], P('seq'), may hold values from -2 to 2
- w_value: bfloat16 [1024, 1024], P('seq'), may hold values from -0.1875 to 0.1875
- w_out: bfloat16 [1024, 1024], P('seq'), may hold values from -0.1875 to 0.1875
- probe_gain: float32 [1024], replicated, may hold values from 0.1 to 1.9
- probe_queries: bfloat16 [256, 1024], replicated, may hold values from -46 to 46
- key_blocks: int32 [64, 8], P('scan'), parts along dimension 0, may hold values from 0 to 31, as said below
- key_counts: int32 [64], P('scan'), parts along dimension 0, may hold values from 1 to 8, as said below
Outputs:
- layer_out: bfloat16 [8192, 1024], P(('scan', 'seq')), parts along dimension 0
- probe_out: float32 [512, 1024], P(('scan', 'seq')), parts along dimension 0
There are 2 independent parts, one for each index of `scan`. A program takes and returns all parts, laid end to end along the dimension named above; an argument that names none is the same for every part. Nothing has to cross between parts.
Inputs may be any that keep to these rules, and one draw needn't show every extreme that they name: `key_blocks`: entry 0 of each query block's list is that block itself; the entries of one list are different blocks. Entries at or after key_counts are ignored. `key_counts`: some block uses all 8 entries in every draw.
All inputs are finite; a program needn't handle non-finite values.
Results may differ from a plain program's by a relative error of at most 0.0061.
Values may be sent and summed in bfloat16 or wider, within the bound.
No kernel may reach another device: no remote copies, remote signals or barrier semaphores. Data moves between devices by JAX's collectives and lax.ppermute only.
A program may use at most 64 MiB of HBM per device.

v0:
```python
import math
import jax
import jax.numpy as jnp
from jax import lax
from jax.sharding import PartitionSpec as P

D = 1024
HEADS = 16
HEAD_DIM = 64
PROBES = 256
BLOCK = 128
MAXK = 8
TOK_DEV = 256
EPS = 1e-05


def layer_norm(values, gain):
    wide = values.astype(jnp.float32)
    center = wide - jnp.mean(wide, axis=-1, keepdims=True)
    spread = jnp.mean(center * center, axis=-1, keepdims=True)
    return (center * lax.rsqrt(spread + EPS) * gain).astype(jnp.bfloat16)


def widen_heads(factor):
    return jnp.repeat(jnp.transpose(factor), HEAD_DIM, axis=1)


def per_device(
    tokens,
    ln_gain,
    w_query,
    w_key,
    w_value,
    w_out,
    probe_gain,
    probe_queries,
    key_blocks,
    key_counts,
):
    scale = 1.0 / math.sqrt(HEAD_DIM)
    ranks = lax.axis_size("seq")
    group = ranks // HEADS
    piece_rows = TOK_DEV // group
    myself = lax.axis_index("seq")
    quarter = myself % group
    normed = layer_norm(tokens, ln_gain)
    columns = normed
    query = jnp.dot(
        columns,
        lax.all_gather(w_query, "seq", axis=0, tiled=True),
        preferred_element_type=jnp.float32,
    )
    keys = jnp.dot(
        columns,
        lax.all_gather(w_key, "seq", axis=0, tiled=True),
        preferred_element_type=jnp.float32,
    )
    values = jnp.dot(
        columns,
        lax.all_gather(w_value, "seq", axis=0, tiled=True),
        preferred_element_type=jnp.float32,
    )
    query = query.astype(jnp.bfloat16)
    pairs = jnp.concatenate(
        [
            keys.astype(jnp.bfloat16).reshape(TOK_DEV, HEADS, HEAD_DIM),
            values.astype(jnp.bfloat16).reshape(TOK_DEV, HEADS, HEAD_DIM),
        ],
        axis=2,
    )
    query_send = jnp.transpose(
        query.reshape(group, piece_rows, HEADS, HEAD_DIM), (2, 0, 1, 3)
    ).reshape(ranks, piece_rows * HEAD_DIM)
    pair_send = jnp.repeat(
        jnp.transpose(pairs, (1, 0, 2)).reshape(HEADS, TOK_DEV * 2 * HEAD_DIM), group, axis=0
    )
    query_got, pair_got = (
        lax.all_to_all(query_send, "seq", split_axis=0, concat_axis=0, tiled=True),
        lax.all_to_all(pair_send, "seq", split_axis=0, concat_axis=0, tiled=True),
    )
    pair_all = pair_got.reshape(ranks * TOK_DEV, 2 * HEAD_DIM)
    blocks_total = ranks * TOK_DEV // BLOCK
    pair_grid = pair_all.reshape(blocks_total, BLOCK, 2 * HEAD_DIM)
    unit = min(piece_rows, BLOCK)
    per_piece = piece_rows // unit
    units = ranks * per_piece
    unit_ids = jnp.arange(units, dtype=jnp.int32)
    starts = unit_ids // per_piece * TOK_DEV + quarter * piece_rows + unit_ids % per_piece * unit
    block_ids = starts // BLOCK
    unit_lists = key_blocks[block_ids]
    unit_counts = key_counts[block_ids]
    per_batch = min(units, max(1, 1024 // unit))
    batches = units // per_batch
    query_units = query_got.reshape(batches, per_batch, unit, HEAD_DIM)
    slot_of = jnp.arange(MAXK * BLOCK, dtype=jnp.int32) // BLOCK

    def attend_batch(operands):
        batch_query, batch_lists, batch_counts = operands
        picked = pair_grid[batch_lists].reshape(per_batch, MAXK * BLOCK, 2 * HEAD_DIM)
        batch_keys = picked[:, :, :HEAD_DIM]
        batch_values = picked[:, :, HEAD_DIM:]
        scores = (
            jnp.einsum("uqd,ukd->uqk", batch_query, batch_keys, preferred_element_type=jnp.float32)
            * scale
        )
        valid = slot_of[None, :] < batch_counts[:, None]
        scores = jnp.where(valid[:, None, :], scores, -jnp.inf)
        top = jnp.max(scores, axis=-1, keepdims=True)
        weights = jnp.exp(scores - top)
        total = jnp.sum(weights, axis=-1, keepdims=True)
        mixed = jnp.einsum(
            "uqk,ukd->uqd",
            weights.astype(jnp.bfloat16),
            batch_values,
            preferred_element_type=jnp.float32,
        )
        return (mixed / total).astype(jnp.bfloat16)

    attended_heads = lax.map(
        attend_batch,
        (
            query_units,
            unit_lists.reshape(batches, per_batch, MAXK),
            unit_counts.reshape(batches, per_batch),
        ),
    )
    returned = lax.all_to_all(
        attended_heads.reshape(ranks, piece_rows * HEAD_DIM),
        "seq",
        split_axis=0,
        concat_axis=0,
        tiled=True,
    )
    attended = jnp.transpose(
        returned.reshape(HEADS, group, piece_rows, HEAD_DIM), (1, 2, 0, 3)
    ).reshape(TOK_DEV, D)
    columns = attended
    projected = jnp.dot(
        columns,
        lax.all_gather(w_out, "seq", axis=0, tiled=True),
        preferred_element_type=jnp.float32,
    )
    layer_out = (tokens.astype(jnp.float32) + projected).astype(jnp.bfloat16)
    pooled = layer_norm(layer_out, probe_gain)
    pooled_heads = pooled.reshape(TOK_DEV, HEADS, HEAD_DIM)
    probe_heads = probe_queries.reshape(PROBES, HEADS, HEAD_DIM)
    probe_scores = (
        jnp.einsum("phd,nhd->hpn", probe_heads, pooled_heads, preferred_element_type=jnp.float32)
        * scale
    )
    pooled_wide = pooled_heads.astype(jnp.float32)
    own_top = jnp.max(probe_scores, axis=-1)
    top = lax.pmax(own_top, "seq")
    weights = jnp.exp(probe_scores - top[:, :, None])
    own_total = jnp.sum(weights, axis=-1)
    own_acc = jnp.einsum(
        "hpn,nhd->phd", weights, pooled_wide, precision=lax.Precision.HIGHEST
    ).reshape(PROBES, D)
    total, accum = lax.psum((own_total, own_acc), "seq")
    probe_all = accum / widen_heads(total)
    share = PROBES // ranks
    probe_out = lax.dynamic_slice_in_dim(probe_all, myself * share, share, 0)
    return (layer_out, probe_out)


def solution(mesh):
    return jax.shard_map(
        per_device,
        mesh=mesh,
        in_specs=(
            P(("scan", "seq"), None),
            P(),
            P("seq", None),
            P("seq", None),
            P("seq", None),
            P("seq", None),
            P(),
            P(),
            P("scan", None),
            P("scan"),
        ),
        out_specs=(P(("scan", "seq"), None), P(("scan", "seq"), None)),
        check_vma=False,
    )
```

profile of v0, /device:TPU:0, one launch (start us, length us, event | category | flops | bytes accessed | tf_op | source)
XLA Modules:
  0.0 426.3 jit_solution(11318317714799748280)
XLA Ops:
  9.4 1.2 convert_reduce_fusion
  10.6 1.3 fusion.54
  11.9 42.4 %all-gather.5.cloned.1.call-done = bf16[1024,1024]{1,0:T(8,128)(2,1)} async-done(((bf16[64,1024]{1,0:T(8,128)(2,1)}), bf16[1024,1024]{1,0:T(8,128)(2,1)}) %all-gather.5.cloned.1.call-update) | async-done | bytes 2097168 | tf_op jit(solution)/shard_map/all_gather | solution.py:50
  54.3 2.5 convolution_convert_fusion.2
  58.7 3.8 reduce.3
  62.6 1.2 reshape.298
  63.8 4.8 %all-to-all-start = ((bf16[16,2,8192]{2,1,0:T(2,128)(2,1)}), bf16[16,2,8192]{2,1,0:T(2,128)(2,1)}, u32[]{:S(2)}, u32[]{:S(2)}) async-start(bf16[16,2,8192]{2,1,0:T(2,128)(2,1)} %reshape.298), calls=%async_computation | async-start | bytes 1048576 | tf_op jit(solution)/shard_map/all_to_all | solution.py:78
  68.5 30.6 %all-gather.7.cloned.1.call-done = bf16[1024,1024]{1,0:T(8,128)(2,1)} async-done(((bf16[64,1024]{1,0:T(8,128)(2,1)}), bf16[1024,1024]{1,0:T(8,128)(2,1)}) %all-gather.7.cloned.1.call-update) | async-done | bytes 2097168 | tf_op jit(solution)/shard_map/all_gather | solution.py:55
  99.1 2.4 convolution_convert_fusion.1
  101.7 39.8 %all-gather.9.cloned.1.call-done = bf16[1024,1024]{1,0:T(8,128)(2,1)} async-done(((bf16[64,1024]{1,0:T(8,128)(2,1)}), bf16[1024,1024]{1,0:T(8,128)(2,1)}) %all-gather.9.cloned.1.call-update) | async-done | bytes 2097168 | tf_op jit(solution)/shard_map/all_gather | solution.py:60
  141.5 2.4 convolution_convert_fusion
  145.4 7.2 %reduce.4 = bf16[16,32768]{1,0:T(8,128)(2,1)S(1)} reduce(bf16[16,1,32768]{2,1,0:T(2,128)(2,1)S(1)} %all_to_all.25, bf16[]{:T(256)} %broadcast.287), dimensions={1}, to_apply=%all_to_all.25.reduce_sub_computation | reduce | bytes 2097154 | tf_op jit(solution)/shard_map/all_to_all | solution.py:79
  152.6 1.6 reshape.300
  154.2 3.7 all-to-all-start.1
  159.9 2.4 reshape.299
  162.3 3.3 reduce
  165.6 1.1 reshape.255
  166.8 1.1 copy.61
  167.9 15.6 %all-to-all-done.1 = bf16[16,2,16384]{2,1,0:T(2,128)(2,1)S(1)} async-done(((bf16[16,2,16384]{2,1,0:T(2,128)(2,1)}), bf16[16,2,16384]{2,1,0:T(2,128)(2,1)S(1)}, u32[]{:S(2)}, u32[]{:S(2)}) %all-to-all-start.1) | async-done | bytes 1048608 | tf_op jit(solution)/shard_map/all_to_all | solution.py:79
  184.5 6.7 %reduce.1 = bf16[16,32768]{1,0:T(8,128)(2,1)S(1)} reduce(bf16[16,1,32768]{2,1,0:T(2,128)(2,1)S(1)} %reshape.301, bf16[]{:T(256)} %constant.115), dimensions={1}, to_apply=%all_to_all.21.reduce_sub_computation | reduce | bytes 2097154 | tf_op jit(solution)/shard_map/all_to_all | solution.py:79
  191.7 27.2 %while.11 = (s32[]{:T(128)}, bf16[4,8,128,64]{2,3,1,0:T(8,128)(2,1)}, s32[4,8]{1,0:T(4,128)S(1)}, bf16[4,8,128,64]{2,3,1,0:T(8,128)(2,1)}, s32[4,8,8]{2,1,0:T(8,...) while((s32[]{:T(128)}, bf16[4,8,128,64]{2,3,1,0:T(8,128)(2,1)}, s32[4,8]{1,0:T(4,128)S(1)}, ...), condition=%wide.region_5.6_spmd.clone, body=%wide.region_2.5_spmd.clone.sunk | while | flops 280116416 | bytes 21301940 | solution.py:119
  193.1 1.8 fusion.85
  194.9 1.1 fusion.86
  196.0 2.7 fusion.87
  199.9 1.8 fusion.85
  201.6 1.1 fusion.86
  202.7 2.7 fusion.87
  206.6 1.8 fusion.85
  208.4 1.1 fusion.86
  209.5 2.7 fusion.87
  213.4 1.8 fusion.85
  215.1 1.1 fusion.86
  216.3 2.7 fusion.87
  219.0 1.6 copy.62
  221.2 3.8 reduce.5
  225.1 1.2 reshape.302
  226.3 8.5 %all-to-all-start.2 = ((bf16[16,2,8192]{2,1,0:T(2,128)(2,1)}), bf16[16,2,8192]{2,1,0:T(2,128)(2,1)S(1)}, u32[]{:S(2)}, u32[]{:S(2)}) async-start(bf16[16,2,8192]{2,1,0:T(2,128)(2,1)} %reshape.302), calls=%async_computation.2 | async-start | bytes 1048576 | tf_op jit(solution)/shard_map/all_to_all | solution.py:127
  235.0 14.2 %all-to-all-done.2 = bf16[16,2,8192]{2,1,0:T(2,128)(2,1)S(1)} async-done(((bf16[16,2,8192]{2,1,0:T(2,128)(2,1)}), bf16[16,2,8192]{2,1,0:T(2,128)(2,1)S(1)}, u32[]{:S(2)}, u32[]{:S(2)}) %all-to-all-start.2) | async-done | bytes 524320 | tf_op jit(solution)/shard_map/all_to_all | solution.py:127
  250.0 3.3 reduce.2
  253.3 1.1 reshape.259
  254.9 2.4 convert_reduce_fusion.1
  258.1 2.7 bitcast_reduce_fusion
  260.8 60.1 %pmax.7 = f32[16,256]{1,0:T(8,128)S(1)} all-reduce(f32[16,256]{1,0:T(8,128)S(1)} %get-tuple-element.94), channel_id=1, replica_groups=mesh['scan'=2,'seq'=16] {'seq'}, use_global_device_ids=true, to_apply=%region_9.10 | all-reduce | flops 4096 | bytes 32768 | tf_op jit(solution)/shard_map/pmax | solution.py:153
  320.9 5.4 %fusion.45 = f32[16,64,256]{2,1,0:T(8,128)} fusion(bf16[256,16,64]{0,2,1:T(8,128)(2,1)S(1)} %bitcast.70, f32[16,256,256]{2,1,0:T(8,128)} %get-tuple-element.95, f32[16,256]{1,0:T(8,128)S(1)} %pmax.7), kind=kOutput, calls=%fused_computation.42 | convolution fusion | flops 807403520 | bytes 5783552 | tf_op jit(solution)/shard_map/hpn,nhd->phd/dot_general | solution.py:156
  326.4 2.9 fusion.44
  329.3 58.1 %psum.15 = f32[256,16]{0,1:T(8,128)S(1)} all-reduce(f32[256,16]{0,1:T(8,128)S(1)} %bitcast.80), channel_id=1, replica_groups=mesh['scan'=2,'seq'=16] {'seq'}, use_global_device_ids=true, to_apply=%region_12.13 | all-reduce | flops 4096 | bytes 32768 | tf_op jit(solution)/shard_map/psum | solution.py:159
  387.4 29.6 %all-reduce.2.cloned.1.call-done = f32[256,1024]{0,1:T(8,128)} async-done(((f32[256,1024]{0,1:T(8,128)}), f32[256,1024]{0,1:T(8,128)}) %all-reduce.2.cloned.1.call-update) | async-done | bytes 1048592 | tf_op jit(solution)/shard_map/psum | solution.py:159
  417.1 1.4 dynamic-slice_divide_fusion
  (87 shorter events, 17.6 us)
Async XLA Ops:
  7.2 152.0 %copy-start = (s32[32]{0:T(128)S(1)}, s32[32]{0:T(128)}, u32[]{:S(2)}) copy-start(s32[32]{0:T(128)} %param.21) | copy-start | bytes 388
  7.2 47.1 %all-gather.5.cloned.1.call-start = ((), (), s32[]{:S(2)}) async-start(), calls=%async_computation.3 | async-start | bytes 2228224 | tf_op jit(solution)/shard_map/all_gather | solution.py:50
  7.9 91.2 %all-gather.7.cloned.1.call-start = ((), (), s32[]{:S(2)}) async-start(), calls=%async_computation.4 | async-start | bytes 2228224 | tf_op jit(solution)/shard_map/all_gather | solution.py:55
  8.7 132.8 %all-gather.9.cloned.1.call-start = ((), (), s32[]{:S(2)}) async-start(), calls=%async_computation.5 | async-start | bytes 2228224 | tf_op jit(solution)/shard_map/all_gather | solution.py:60
  56.9 42.3 %copy-start.1 = (bf16[256,1024]{1,0:T(8,128)(2,1)S(1)}, bf16[256,1024]{1,0:T(8,128)(2,1)}, u32[]{:S(2)}) copy-start(bf16[256,1024]{1,0:T(8,128)(2,1)} %param.12) | copy-start | bytes 1572868
  56.9 42.3 %copy-start.7 = (f32[1024]{0:T(1024)S(1)}, f32[1024]{0:T(1024)}, u32[]{:S(2)}) copy-start(f32[1024]{0:T(1024)} %param.13) | copy-start | bytes 12292
  63.8 90.4 %all-to-all-start = ((bf16[16,2,8192]{2,1,0:T(2,128)(2,1)}), bf16[16,2,8192]{2,1,0:T(2,128)(2,1)}, u32[]{:S(2)}, u32[]{:S(2)}) async-start(bf16[16,2,8192]{2,1,0:T(2,128)(2,1)} %reshape.298), calls=%async_computation | async-start | bytes 1048576 | tf_op jit(solution)/shard_map/all_to_all | solution.py:78
  145.3 13.1 %copy-start.6 = (s32[32,8]{0,1:T(8,128)S(1)}, s32[32,8]{0,1:T(8,128)}, u32[]{:S(2)}) copy-start(s32[32,8]{0,1:T(8,128)} %param.20) | copy-start | bytes 3076
  154.2 29.3 %all-to-all-start.1 = ((bf16[16,2,16384]{2,1,0:T(2,128)(2,1)}), bf16[16,2,16384]{2,1,0:T(2,128)(2,1)S(1)}, u32[]{:S(2)}, u32[]{:S(2)}) async-start(bf16[16,2,16384]{2,1,0:T(2,128)(2,1)} %reshape.300), calls=%async_computation.1 | async-start | bytes 2097152 | tf_op jit(solution)/shard_map/all_to_all | solution.py:79
  157.9 97.0 %all-gather.11.cloned.1.call-start = ((), (), s32[]{:S(2)}) async-start(), calls=%async_computation.6 | async-start | bytes 2228224 | tf_op jit(solution)/shard_map/all_gather | solution.py:140
  219.0 15.9 %copy-start.4 = (bf16[256,1024]{1,0:T(8,128)(2,1)S(1)}, bf16[256,1024]{1,0:T(8,128)(2,1)}, u32[]{:S(2)}) copy-start(bf16[256,1024]{1,0:T(8,128)(2,1)} %param.19) | copy-start | bytes 1572868
  226.3 28.6 %copy-start.2 = (bf16[256,1024]{1,0:T(8,128)(2,1)S(1)}, bf16[256,1024]{1,0:T(8,128)(2,1)}, u32[]{:S(2)}) copy-start(bf16[256,1024]{1,0:T(8,128)(2,1)} %param.12) | copy-start | bytes 1572868
  226.3 23.0 %all-to-all-start.2 = ((bf16[16,2,8192]{2,1,0:T(2,128)(2,1)}), bf16[16,2,8192]{2,1,0:T(2,128)(2,1)S(1)}, u32[]{:S(2)}, u32[]{:S(2)}) async-start(bf16[16,2,8192]{2,1,0:T(2,128)(2,1)} %reshape.302), calls=%async_computation.2 | async-start | bytes 1048576 | tf_op jit(solution)/shard_map/all_to_all | solution.py:127
  234.8 182.3 %all-reduce.2.cloned.1.call-start = ((), (), s32[]{:S(2)}) async-start(), calls=%async_computation.7 | async-start | bytes 2097152 | tf_op jit(solution)/shard_map/psum | solution.py:159
  250.0 7.6 %copy-start.5 = (f32[1024]{0:T(1024)S(1)}, f32[1024]{0:T(1024)}, u32[]{:S(2)}) copy-start(f32[1024]{0:T(1024)} %param.18) | copy-start | bytes 12292
  257.3 69.1 %copy-start.3 = (bf16[256,1024]{1,0:T(8,128)(2,1)}, bf16[256,1024]{1,0:T(8,128)(2,1)S(1)}, u32[]{:S(2)}) copy-start(bf16[256,1024]{1,0:T(8,128)(2,1)S(1)} %get-tuple-element.93) | copy-start | bytes 1572868
Sparse Core Ops, SparseCore 0:
  10.2 44.0 all-gather.4
  56.5 42.6 all-gather.6
  101.3 40.1 all-gather.8
  160.6 48.5 all-gather.10
  326.5 90.4 all-reduce.1
where the time goes:
time: 432 us; the launch traced here: 426 us
  waiting for transfers between devices  175 us (41%)
  blocking collectives  118 us (27%)
  other arithmetic  40.5 us (9%)
  matrix products  35.7 us (8%)
  local copies, waits for them, and re-layouts  25 us (6%)
  starting transfers between devices  17.1 us (4%)
  between operations  14.6 us (3%)
    pmax x1, blocking collectives, per_device(): top = lax.pmax(own_top, 'seq')  60.1 us
    psum x1, blocking collectives, per_device(): total, accum = lax.psum((own_total, own_acc), 'seq')  58.1 us
    all_gather x1, waiting for transfers between devices, per_device(): lax.all_gather(w_query, 'seq', axis=0, tiled=True)  42.4 us
    all_gather x1, waiting for transfers between devices, per_device(): lax.all_gather(w_value, 'seq', axis=0, tiled=True)  39.8 us
    all_gather x1, waiting for transfers between devices, per_device(): lax.all_gather(w_key, 'seq', axis=0, tiled=True)  30.6 us
    psum x1, waiting for transfers between devices, per_device(): total, accum = lax.psum((own_total, own_acc), 'seq')  29.6 us
    all_to_all x1, waiting for transfers between devices, per_device(): lax.all_to_all(pair_send, 'seq', split_axis=0, concat_axis=0, tiled=True)  15.6 us
    all_to_all x1, waiting for transfers between devices, per_device(): lax.all_to_all(attended_heads.reshape(ranks, piece_rows * HEAD_DIM), 'seq...  14.2 us
  transfers between devices with their start and end apart: 8, of which 6 were waited for; matrix products, arithmetic and copies ran while one was open for 20% of the time, Pallas kernels for 0%

commit v1 on v0

--- a/solution.py
+++ b/solution.py
@@ -12,6 +12,30 @@
 MAXK = 8
 TOK_DEV = 256
 EPS = 1e-05
+
+
+def split_up(value, dim, size):
+    shape = value.shape
+    tiles = value.reshape(*shape[:dim], size, shape[dim] // size, *shape[dim + 1 :])
+    return jnp.moveaxis(tiles, dim, 0)
+
+
+def joined_along(tiles, dim):
+    tiles = jnp.moveaxis(tiles, 0, dim)
+    dims = tiles.shape
+    return tiles.reshape(*dims[:dim], dims[dim] * dims[dim + 1], *dims[dim + 2 :])
+
+
+def sent_to_each(value, axis, split_dim, concat_dim):
+    size, index = (lax.axis_size(axis), lax.axis_index(axis))
+    blocks = split_up(value, split_dim, size)
+    out = blocks
+    for turn in range(1, size):
+        target, source = ((index + turn) % size, (index - turn) % size)
+        sent = lax.dynamic_index_in_dim(blocks, target, 0)
+        theirs = lax.ppermute(sent, axis, [(i, (i + turn) % size) for i in range(size)])
+        out = lax.dynamic_update_slice_in_dim(out, theirs, source, axis=0)
+    return joined_along(out, concat_dim)
 
 
 def layer_norm(values, gain):
@@ -124,13 +148,7 @@
             unit_counts.reshape(batches, per_batch),
         ),
     )
-    returned = lax.all_to_all(
-        attended_heads.reshape(ranks, piece_rows * HEAD_DIM),
-        "seq",
-        split_axis=0,
-        concat_axis=0,
-        tiled=True,
-    )
+    returned = sent_to_each(attended_heads.reshape(ranks, piece_rows * HEAD_DIM), "seq", 0, 0)
     attended = jnp.transpose(
         returned.reshape(HEADS, group, piece_rows, HEAD_DIM), (1, 2, 0, 3)
     ).reshape(TOK_DEV, D)

time: 432 us -> 447 us (1.035)
  local copies, waits for them, and re-layouts: 25 us -> 41.8 us
  starting transfers between devices: 17.1 us -> 31.8 us
  waiting for transfers between devices: 175 us -> 168 us
  other arithmetic: 40.5 us -> 33.6 us
    ppermute x0 -> x15, starting transfers between devices: none -> 23.5 us  [sent_to_each(): lax.ppermute(sent, axis, [(i, (i + turn) % size) for i in range(size)])]
    dynamic_update_slice x0 -> x15, local copies, waits for them, and re-layouts: none -> 17.3 us  [sent_to_each(): out = lax.dynamic_update_slice_in_dim(out, theirs, source, axis=0)]
    all_to_all x1 -> x0, waiting for transfers between devices: 14.2 us -> none  [per_device(): lax.all_to_all(attended_heads.reshape(ranks, piece_rows * HEAD_DIM), 'seq...]
    all_gather x1, waiting for transfers between devices: 30.6 us -> 39.8 us  [per_device(): lax.all_gather(w_key, 'seq', axis=0, tiled=True)]
    all_gather x1, waiting for transfers between devices: 39.8 us -> 30.6 us  [per_device(): lax.all_gather(w_value, 'seq', axis=0, tiled=True)]
    all_to_all x1 -> x0, starting transfers between devices: 8.51 us -> none  [per_device(): lax.all_to_all(attended_heads.reshape(ranks, piece_rows * HEAD_DIM), 'seq...]
    ppermute x0 -> x15, waiting for transfers between devices: none -> 7.29 us  [sent_to_each(): lax.ppermute(sent, axis, [(i, (i + turn) % size) for i in range(size)])]
    all_to_all x2 -> x0, other arithmetic: 7.15 us -> none  [per_device(): lax.all_to_all(attended_heads.reshape(ranks, piece_rows * HEAD_DIM), 'seq...]
  transfers between devices with their start and end apart: 8 -> 22, of which waited for: 6 -> 8; matrix products, arithmetic and copies ran while one was open for 20% -> 22% of each run, Pallas kernels for 0% -> 0%
where the time goes in v1:
time: 447 us; the launch traced here: 442 us
  waiting for transfers between devices  168 us (38%)
  blocking collectives  116 us (26%)
  local copies, waits for them, and re-layouts  41.8 us (9%)
  matrix products  35.7 us (8%)
  other arithmetic  33.6 us (8%)
  starting transfers between devices  31.8 us (7%)
  between operations  14.8 us (3%)
    psum x1, blocking collectives, per_device(): total, accum = lax.psum((own_total, own_acc), 'seq')  58.1 us
    pmax x1, blocking collectives, per_device(): top = lax.pmax(own_top, 'seq')  58 us
    all_gather x1, waiting for transfers between devices, per_device(): lax.all_gather(w_query, 'seq', axis=0, tiled=True)  42.4 us
    all_gather x1, waiting for transfers between devices, per_device(): lax.all_gather(w_key, 'seq', axis=0, tiled=True)  39.8 us
    all_gather x1, waiting for transfers between devices, per_device(): lax.all_gather(w_value, 'seq', axis=0, tiled=True)  30.6 us
    psum x1, waiting for transfers between devices, per_device(): total, accum = lax.psum((own_total, own_acc), 'seq')  29.7 us
    ppermute x15, starting transfers between devices, sent_to_each(): lax.ppermute(sent, axis, [(i, (i + turn) % size) for i in range(size)])  23.5 us
    dynamic_update_slice x15, local copies, waits for them, and re-layouts, sent_to_each(): out = lax.dynamic_update_slice_in_dim(out, theirs, source, axis=0)  17.3 us
  transfers between devices with their start and end apart: 22, of which 8 were waited for; matrix products, arithmetic and copies ran while one was open for 22% of the time, Pallas kernels for 0%

profile of v1, /device:TPU:0, one launch (start us, length us, event | category | flops | bytes accessed | tf_op | source)
XLA Modules:
  0.0 441.7 jit_solution(14808259195285282156)
XLA Ops:
  9.4 1.2 convert_reduce_fusion
  10.6 1.3 fusion.54
  11.9 42.4 %all-gather.5.cloned.1.call-done = bf16[1024,1024]{1,0:T(8,128)(2,1)} async-done(((bf16[64,1024]{1,0:T(8,128)(2,1)}), bf16[1024,1024]{1,0:T(8,128)(2,1)}) %all-gather.5.cloned.1.call-update) | async-done | bytes 2097168 | tf_op jit(solution)/shard_map/all_gather | solution.py:74
  54.3 2.5 convolution_convert_fusion.2
  58.8 3.9 reduce.2
  62.7 1.2 reshape.288
  63.9 4.4 all-to-all-start
  68.3 30.6 %all-gather.9.cloned.1.call-done = bf16[1024,1024]{1,0:T(8,128)(2,1)} async-done(((bf16[64,1024]{1,0:T(8,128)(2,1)}), bf16[1024,1024]{1,0:T(8,128)(2,1)}) %all-gather.9.cloned.1.call-update) | async-done | bytes 2097168 | tf_op jit(solution)/shard_map/all_gather | solution.py:84
  98.9 2.4 convolution_convert_fusion
  101.5 39.8 %all-gather.7.cloned.1.call-done = bf16[1024,1024]{1,0:T(8,128)(2,1)} async-done(((bf16[64,1024]{1,0:T(8,128)(2,1)}), bf16[1024,1024]{1,0:T(8,128)(2,1)}) %all-gather.7.cloned.1.call-update) | async-done | bytes 2097168 | tf_op jit(solution)/shard_map/all_gather | solution.py:79
  141.3 2.4 convolution_convert_fusion.1
  145.1 7.3 %reduce.3 = bf16[16,32768]{1,0:T(8,128)(2,1)S(1)} reduce(bf16[16,1,32768]{2,1,0:T(2,128)(2,1)S(1)} %all_to_all.17, bf16[]{:T(256)} %broadcast.316), dimensions={1}, to_apply=%all_to_all.17.reduce_sub_computation | reduce | bytes 2097154 | tf_op jit(solution)/shard_map/all_to_all | solution.py:103
  152.5 1.6 reshape.290
  154.1 3.7 all-to-all-start.1
  160.1 2.4 reshape.289
  162.6 3.3 reduce
  167.0 1.2 copy.60
  168.1 15.2 %all-to-all-done.1 = bf16[16,2,16384]{2,1,0:T(2,128)(2,1)S(1)} async-done(((bf16[16,2,16384]{2,1,0:T(2,128)(2,1)}), bf16[16,2,16384]{2,1,0:T(2,128)(2,1)S(1)}, u32[]{:S(2)}, u32[]{:S(2)}) %all-to-all-start.1) | async-done | bytes 1048608 | tf_op jit(solution)/shard_map/all_to_all | solution.py:103
  184.4 6.7 %reduce.1 = bf16[16,32768]{1,0:T(8,128)(2,1)S(1)} reduce(bf16[16,1,32768]{2,1,0:T(2,128)(2,1)S(1)} %reshape.291, bf16[]{:T(256)} %constant.324), dimensions={1}, to_apply=%all_to_all.15.reduce_sub_computation | reduce | bytes 2097154 | tf_op jit(solution)/shard_map/all_to_all | solution.py:103
  191.6 27.4 %while.11 = (s32[]{:T(128)}, bf16[4,8,128,64]{2,3,1,0:T(8,128)(2,1)}, s32[4,8]{1,0:T(4,128)S(1)}, bf16[4,8,128,64]{2,3,1,0:T(8,128)(2,1)}, s32[4,8,8]{2,1,0:T(8,...) while((s32[]{:T(128)}, bf16[4,8,128,64]{2,3,1,0:T(8,128)(2,1)}, s32[4,8]{1,0:T(4,128)S(1)}, ...), condition=%wide.region_5.6_spmd.clone, body=%wide.region_2.5_spmd.clone.sunk | while | flops 280116416 | bytes 21300932 | solution.py:143
  193.2 1.8 fusion.85
  196.1 2.7 fusion.87
  199.9 1.8 fusion.85
  202.8 2.7 fusion.87
  206.7 1.8 fusion.85
  209.6 2.7 fusion.87
  213.4 1.8 fusion.85
  216.3 2.7 fusion.87
  219.0 1.6 copy.61
  222.6 1.6 collective-permute-start
  224.2 2.6 collective-permute-start.1
  226.8 3.4 collective-permute-start.2
  231.5 1.8 collective-permute-start.5
  233.4 2.9 collective-permute-start.6
  238.3 4.5 %collective-permute-done.4 = bf16[1,1,16384]{2,0,1:T(2,128)(2,1)S(1)} collective-permute-done((bf16[1,1,16384]{2,0,1:T(2,128)(2,1)S(1)}, bf16[1,1,16384]{2,0,1:T(2,128)(2,1)S(1)}, u32[]{:S(2)}, u32[]{:S(2)}) %collective-permute-start.4) | collective-permute-done | bytes 32800 | tf_op jit(solution)/shard_map/ppermute | solution.py:36
  242.8 2.3 collective-permute-done.5
  245.1 4.2 collective-permute-start.11
  249.3 1.5 collective-permute-start.12
  250.8 2.6 collective-permute-start.13
  253.7 1.3 dynamic_update_slice.49
  272.7 2.4 convert_reduce_fusion.1
  276.0 2.7 bitcast_reduce_fusion
  278.7 58.0 %pmax.7 = f32[16,256]{1,0:T(8,128)S(1)} all-reduce(f32[16,256]{1,0:T(8,128)S(1)} %get-tuple-element.109), channel_id=1, replica_groups=mesh['scan'=2,'seq'=16] {'seq'}, use_global_device_ids=true, to_apply=%region_9.10 | all-reduce | flops 4096 | bytes 32768 | tf_op jit(solution)/shard_map/pmax | solution.py:171
  336.6 5.4 %fusion.45 = f32[16,64,256]{2,1,0:T(8,128)} fusion(bf16[256,16,64]{0,2,1:T(8,128)(2,1)S(1)} %bitcast.72, f32[16,256,256]{2,1,0:T(8,128)} %get-tuple-element.110, f32[16,256]{1,0:T(8,128)S(1)} %pmax.7), kind=kOutput, calls=%fused_computation.42 | convolution fusion | flops 807403520 | bytes 5783552 | tf_op jit(solution)/shard_map/hpn,nhd->phd/dot_general | solution.py:174
  342.1 2.9 fusion.44
  345.0 58.1 %psum.15 = f32[256,16]{0,1:T(8,128)S(1)} all-reduce(f32[256,16]{0,1:T(8,128)S(1)} %bitcast.82), channel_id=1, replica_groups=mesh['scan'=2,'seq'=16] {'seq'}, use_global_device_ids=true, to_apply=%region_12.13 | all-reduce | flops 4096 | bytes 32768 | tf_op jit(solution)/shard_map/psum | solution.py:177
  403.1 29.7 %all-reduce.2.cloned.1.call-done = f32[256,1024]{0,1:T(8,128)} async-done(((f32[256,1024]{0,1:T(8,128)}), f32[256,1024]{0,1:T(8,128)}) %all-reduce.2.cloned.1.call-update) | async-done | bytes 1048592 | tf_op jit(solution)/shard_map/psum | solution.py:177
  432.8 1.4 dynamic-slice_divide_fusion
  (127 shorter events, 44.3 us)
Async XLA Ops:
  7.2 151.4 %copy-start = (s32[32]{0:T(128)S(1)}, s32[32]{0:T(128)}, u32[]{:S(2)}) copy-start(s32[32]{0:T(128)} %param.21) | copy-start | bytes 388
  7.2 47.1 %all-gather.5.cloned.1.call-start = ((), (), s32[]{:S(2)}) async-start(), calls=%async_computation.2 | async-start | bytes 2228224 | tf_op jit(solution)/shard_map/all_gather | solution.py:74
  7.9 91.0 %all-gather.9.cloned.1.call-start = ((), (), s32[]{:S(2)}) async-start(), calls=%async_computation.4 | async-start | bytes 2228224 | tf_op jit(solution)/shard_map/all_gather | solution.py:84
  8.7 132.6 %all-gather.7.cloned.1.call-start = ((), (), s32[]{:S(2)}) async-start(), calls=%async_computation.3 | async-start | bytes 2228224 | tf_op jit(solution)/shard_map/all_gather | solution.py:79
  56.9 42.1 %copy-start.1 = (bf16[256,1024]{1,0:T(8,128)(2,1)S(1)}, bf16[256,1024]{1,0:T(8,128)(2,1)}, u32[]{:S(2)}) copy-start(bf16[256,1024]{1,0:T(8,128)(2,1)} %param.12) | copy-start | bytes 1572868
  56.9 42.1 %copy-start.7 = (f32[1024]{0:T(1024)S(1)}, f32[1024]{0:T(1024)}, u32[]{:S(2)}) copy-start(f32[1024]{0:T(1024)} %param.13) | copy-start | bytes 12292
  63.9 90.2 %all-to-all-start = ((bf16[16,2,8192]{2,1,0:T(2,128)(2,1)}), bf16[16,2,8192]{2,1,0:T(2,128)(2,1)}, u32[]{:S(2)}, u32[]{:S(2)}) async-start(bf16[16,2,8192]{2,1,0:T(2,128)(2,1)} %reshape.288), calls=%async_computation | async-start | bytes 1048576 | tf_op jit(solution)/shard_map/all_to_all | solution.py:102
  145.1 14.2 %copy-start.6 = (s32[32,8]{0,1:T(8,128)S(1)}, s32[32,8]{0,1:T(8,128)}, u32[]{:S(2)}) copy-start(s32[32,8]{0,1:T(8,128)} %param.20) | copy-start | bytes 3076
  154.1 29.3 %all-to-all-start.1 = ((bf16[16,2,16384]{2,1,0:T(2,128)(2,1)}), bf16[16,2,16384]{2,1,0:T(2,128)(2,1)S(1)}, u32[]{:S(2)}, u32[]{:S(2)}) async-start(bf16[16,2,16384]{2,1,0:T(2,128)(2,1)} %reshape.290), calls=%async_computation.1 | async-start | bytes 2097152 | tf_op jit(solution)/shard_map/all_to_all | solution.py:103
  157.7 115.0 %all-gather.11.cloned.1.call-start = ((), (), s32[]{:S(2)}) async-start(), calls=%async_computation.5 | async-start | bytes 2228224 | tf_op jit(solution)/shard_map/all_gather | solution.py:158
  158.3 274.4 %all-reduce.2.cloned.1.call-start = ((), (), s32[]{:S(2)}) async-start(), calls=%async_computation.6 | async-start | bytes 2097152 | tf_op jit(solution)/shard_map/psum | solution.py:177
  219.0 34.4 %copy-start.4 = (bf16[256,1024]{1,0:T(8,128)(2,1)S(1)}, bf16[256,1024]{1,0:T(8,128)(2,1)}, u32[]{:S(2)}) copy-start(bf16[256,1024]{1,0:T(8,128)(2,1)} %param.19) | copy-start | bytes 1572868
  221.4 51.3 %copy-start.2 = (bf16[256,1024]{1,0:T(8,128)(2,1)S(1)}, bf16[256,1024]{1,0:T(8,128)(2,1)}, u32[]{:S(2)}) copy-start(bf16[256,1024]{1,0:T(8,128)(2,1)} %param.12) | copy-start | bytes 1572868
  222.6 9.0 %collective-permute-start = (bf16[1,1,16384]{2,0,1:T(2,128)(2,1)S(1)}, bf16[1,1,16384]{2,0,1:T(2,128)(2,1)S(1)}, u32[]{:S(2)}, u32[]{:S(2)}) collective-permute-start(bf16[1,1,16384]{2,0,1:T(2,128)(2,1)S(1)} %get-tuple-element.106), channel_id=1, source_target_pairs={{0,1},{1,2},{2,3},{3,4},{4,5},{5,6},{6,7},{7,8},{8,9},{9,10},{10,1... | collective-permute-start | bytes 98312 | tf_op jit(solution)/shard_map/ppermute | solution.py:36
  224.2 9.2 %collective-permute-start.1 = (bf16[1,1,16384]{2,0,1:T(2,128)(2,1)S(1)}, bf16[1,1,16384]{2,0,1:T(2,128)(2,1)S(1)}, u32[]{:S(2)}, u32[]{:S(2)}) collective-permute-start(bf16[1,1,16384]{2,0,1:T(2,128)(2,1)S(1)} %get-tuple-element.105), channel_id=1, source_target_pairs={{0,2},{1,3},{2,4},{3,5},{4,6},{5,7},{6,8},{7,9},{8,10},{9,11},{10,... | collective-permute-start | bytes 98312 | tf_op jit(solution)/shard_map/ppermute | solution.py:36
  226.8 9.5 %collective-permute-start.2 = (bf16[1,1,16384]{2,0,1:T(2,128)(2,1)S(1)}, bf16[1,1,16384]{2,0,1:T(2,128)(2,1)S(1)}, u32[]{:S(2)}, u32[]{:S(2)}) collective-permute-start(bf16[1,1,16384]{2,0,1:T(2,128)(2,1)S(1)} %get-tuple-element.104), channel_id=1, source_target_pairs={{0,3},{1,4},{2,5},{3,6},{4,7},{5,8},{6,9},{7,10},{8,11},{9,12},{10... | collective-permute-start | bytes 98312 | tf_op jit(solution)/shard_map/ppermute | solution.py:36
  230.2 7.2 %collective-permute-start.3 = (bf16[1,1,16384]{2,0,1:T(2,128)(2,1)S(1)}, bf16[1,1,16384]{2,0,1:T(2,128)(2,1)S(1)}, u32[]{:S(2)}, u32[]{:S(2)}) collective-permute-start(bf16[1,1,16384]{2,0,1:T(2,128)(2,1)S(1)} %get-tuple-element.103), channel_id=1, source_target_pairs={{0,4},{1,5},{2,6},{3,7},{4,8},{5,9},{6,10},{7,11},{8,12},{9,13},{1... | collective-permute-start | bytes 98312 | tf_op jit(solution)/shard_map/ppermute | solution.py:36
  230.9 11.8 %collective-permute-start.4 = (bf16[1,1,16384]{2,0,1:T(2,128)(2,1)S(1)}, bf16[1,1,16384]{2,0,1:T(2,128)(2,1)S(1)}, u32[]{:S(2)}, u32[]{:S(2)}) collective-permute-start(bf16[1,1,16384]{2,0,1:T(2,128)(2,1)S(1)} %get-tuple-element.102), channel_id=1, source_target_pairs={{0,5},{1,6},{2,7},{3,8},{4,9},{5,10},{6,11},{7,12},{8,13},{9,14},{... | collective-permute-start | bytes 98312 | tf_op jit(solution)/shard_map/ppermute | solution.py:36
  231.5 13.6 %collective-permute-start.5 = (bf16[1,1,16384]{2,0,1:T(2,128)(2,1)S(1)}, bf16[1,1,16384]{2,0,1:T(2,128)(2,1)S(1)}, u32[]{:S(2)}, u32[]{:S(2)}) collective-permute-start(bf16[1,1,16384]{2,0,1:T(2,128)(2,1)S(1)} %get-tuple-element.101), channel_id=1, source_target_pairs={{0,6},{1,7},{2,8},{3,9},{4,10},{5,11},{6,12},{7,13},{8,14},{9,15},... | collective-permute-start | bytes 98312 | tf_op jit(solution)/shard_map/ppermute | solution.py:36
  233.4 11.7 %collective-permute-start.6 = (bf16[1,1,16384]{2,0,1:T(2,128)(2,1)S(1)}, bf16[1,1,16384]{2,0,1:T(2,128)(2,1)S(1)}, u32[]{:S(2)}, u32[]{:S(2)}) collective-permute-start(bf16[1,1,16384]{2,0,1:T(2,128)(2,1)S(1)} %get-tuple-element.100), channel_id=1, source_target_pairs={{0,7},{1,8},{2,9},{3,10},{4,11},{5,12},{6,13},{7,14},{8,15},{9,0},... | collective-permute-start | bytes 98312 | tf_op jit(solution)/shard_map/ppermute | solution.py:36
  236.3 13.0 %collective-permute-start.7 = (bf16[1,1,16384]{2,0,1:T(2,128)(2,1)S(1)}, bf16[1,1,16384]{2,0,1:T(2,128)(2,1)S(1)}, u32[]{:S(2)}, u32[]{:S(2)}) collective-permute-start(bf16[1,1,16384]{2,0,1:T(2,128)(2,1)S(1)} %get-tuple-element.99), channel_id=1, source_target_pairs={{0,8},{1,9},{2,10},{3,11},{4,12},{5,13},{6,14},{7,15},{8,0},{9,1},... | collective-permute-start | bytes 98312 | tf_op jit(solution)/shard_map/ppermute | solution.py:36
  237.3 13.5 %collective-permute-start.8 = (bf16[1,1,16384]{2,0,1:T(2,128)(2,1)S(1)}, bf16[1,1,16384]{2,0,1:T(2,128)(2,1)S(1)}, u32[]{:S(2)}, u32[]{:S(2)}) collective-permute-start(bf16[1,1,16384]{2,0,1:T(2,128)(2,1)S(1)} %get-tuple-element.98), channel_id=1, source_target_pairs={{0,9},{1,10},{2,11},{3,12},{4,13},{5,14},{6,15},{7,0},{8,1},{9,2},... | collective-permute-start | bytes 98312 | tf_op jit(solution)/shard_map/ppermute | solution.py:36
  242.8 10.6 %collective-permute-start.9 = (bf16[1,1,16384]{2,0,1:T(2,128)(2,1)S(1)}, bf16[1,1,16384]{2,0,1:T(2,128)(2,1)S(1)}, u32[]{:S(2)}, u32[]{:S(2)}) collective-permute-start(bf16[1,1,16384]{2,0,1:T(2,128)(2,1)S(1)} %get-tuple-element.97), channel_id=1, source_target_pairs={{0,10},{1,11},{2,12},{3,13},{4,14},{5,15},{6,0},{7,1},{8,2},{9,3},... | collective-permute-start | bytes 98312 | tf_op jit(solution)/shard_map/ppermute | solution.py:36
  245.1 20.3 %collective-permute-start.10 = (bf16[1,1,16384]{2,0,1:T(2,128)(2,1)S(1)}, bf16[1,1,16384]{2,0,1:T(2,128)(2,1)S(1)}, u32[]{:S(2)}, u32[]{:S(2)}) collective-permute-start(bf16[1,1,16384]{2,0,1:T(2,128)(2,1)S(1)} %get-tuple-element.96), channel_id=1, source_target_pairs={{0,11},{1,12},{2,13},{3,14},{4,15},{5,0},{6,1},{7,2},{8,3},{9,4},{... | collective-permute-start | bytes 98312 | tf_op jit(solution)/shard_map/ppermute | solution.py:36
  245.1 21.5 %collective-permute-start.11 = (bf16[1,1,16384]{2,0,1:T(2,128)(2,1)S(1)}, bf16[1,1,16384]{2,0,1:T(2,128)(2,1)S(1)}, u32[]{:S(2)}, u32[]{:S(2)}) collective-permute-start(bf16[1,1,16384]{2,0,1:T(2,128)(2,1)S(1)} %get-tuple-element.95), channel_id=1, source_target_pairs={{0,12},{1,13},{2,14},{3,15},{4,0},{5,1},{6,2},{7,3},{8,4},{9,5},{1... | collective-permute-start | bytes 98312 | tf_op jit(solution)/shard_map/ppermute | solution.py:36
  249.3 18.4 %collective-permute-start.12 = (bf16[1,1,16384]{2,0,1:T(2,128)(2,1)S(1)}, bf16[1,1,16384]{2,0,1:T(2,128)(2,1)S(1)}, u32[]{:S(2)}, u32[]{:S(2)}) collective-permute-start(bf16[1,1,16384]{2,0,1:T(2,128)(2,1)S(1)} %get-tuple-element.94), channel_id=1, source_target_pairs={{0,13},{1,14},{2,15},{3,0},{4,1},{5,2},{6,3},{7,4},{8,5},{9,6},{10... | collective-permute-start | bytes 98312 | tf_op jit(solution)/shard_map/ppermute | solution.py:36
  250.8 18.1 %collective-permute-start.13 = (bf16[1,1,16384]{2,0,1:T(2,128)(2,1)S(1)}, bf16[1,1,16384]{2,0,1:T(2,128)(2,1)S(1)}, u32[]{:S(2)}, u32[]{:S(2)}) collective-permute-start(bf16[1,1,16384]{2,0,1:T(2,128)(2,1)S(1)} %get-tuple-element.93), channel_id=1, source_target_pairs={{0,14},{1,15},{2,0},{3,1},{4,2},{5,3},{6,4},{7,5},{8,6},{9,7},{10,... | collective-permute-start | bytes 98312 | tf_op jit(solution)/shard_map/ppermute | solution.py:36
  253.4 16.6 %collective-permute-start.14 = (bf16[1,1,16384]{2,0,1:T(2,128)(2,1)S(1)}, bf16[1,1,16384]{2,0,1:T(2,128)(2,1)S(1)}, u32[]{:S(2)}, u32[]{:S(2)}) collective-permute-start(bf16[1,1,16384]{2,0,1:T(2,128)(2,1)S(1)} %get-tuple-element.92), channel_id=1, source_target_pairs={{0,15},{1,0},{2,1},{3,2},{4,3},{5,4},{6,5},{7,6},{8,7},{9,8},{10,9... | collective-permute-start | bytes 98312 | tf_op jit(solution)/shard_map/ppermute | solution.py:36
  261.9 13.5 %copy-start.5 = (f32[1024]{0:T(1024)S(1)}, f32[1024]{0:T(1024)}, u32[]{:S(2)}) copy-start(f32[1024]{0:T(1024)} %param.18) | copy-start | bytes 12292
  275.2 66.9 %copy-start.3 = (bf16[256,1024]{1,0:T(8,128)(2,1)}, bf16[256,1024]{1,0:T(8,128)(2,1)S(1)}, u32[]{:S(2)}) copy-start(bf16[256,1024]{1,0:T(8,128)(2,1)S(1)} %get-tuple-element.108) | copy-start | bytes 1572868
Sparse Core Ops, SparseCore 0:
  10.2 44.0 all-gather.4
  56.5 42.3 all-gather.8
  101.1 40.1 all-gather.6
  160.4 48.5 all-gather.10
  342.2 90.4 all-reduce.1
